TPU v7x, 256 devices: a whole 4x4x8 slice. The times are simulated.
256 devices in a mesh: row: 32 (over z_lo, x, core), col: 8 (over z_hi, y).
Axes of the slice: x: 4, y: 4, z: 8 (z_hi: 2, z_lo: 4; z = z_hi * 4 + z_lo), core: 2. Of those that a mesh axis runs over, the one named last changes fastest.
Arguments:
- ancestors: bfloat16 [128, 128, 256, 256], P('row', 'col'), may hold values from -6 to 6
- panel_one: bfloat16 [2, 128, 256, 256], P(None, 'row'), may hold values from -0.0625 to 0.0625
- present_one: int32 [2, 128], replicated, may hold values from 0 to 1, as said below
- dinv_one: bfloat16 [2, 256, 256], replicated, may hold values from -6 to 6
- panel_two: bfloat16 [2, 128, 256, 256], P(None, 'row'), may hold values from -0.0625 to 0.0625
- present_two: int32 [2, 128], replicated, may hold values from 0 to 1, as said below
- dinv_two: bfloat16 [2, 256, 256], replicated, may hold values from -6 to 6
Outputs:
- update_one: float32 [256, 256, 256], P(('row', 'col'))
- diag_one: float32 [2, 256, 256], replicated
- update_two: float32 [256, 256, 256], P(('row', 'col'))
- diag_two: float32 [2, 256, 256], replicated
Inputs may be any that keep to these rules, and one draw needn't show every extreme that they name: `present_one`: each supernode's row has 16 to 64 ones, block row 0 among them; the first supernode of each level has exactly 64. `present_two`: each supernode's row has 16 to 64 ones, block row 0 among them; the first supernode of each level has exactly 64.
All inputs are finite; a program needn't handle non-finite values.
Results may differ from a plain program's by a relative error of at most 0.0003.
Values may be sent and summed in bfloat16 or wider, within the bound.
No kernel may reach another device: no remote copies, remote signals or barrier semaphores. Data moves between devices by JAX's collectives and lax.ppermute only.
A program may use at most 128 MiB of HBM per device.

v0:
```python
import jax
import jax.numpy as jnp
from jax import lax
from jax.sharding import PartitionSpec as P


def spread(block, axis, holder):
    block = jnp.where(lax.axis_index(axis) == holder, block, jnp.zeros_like(block))
    return lax.psum(block, axis)


def one_level(ancestors, panel_part, present, inv_diag):
    a_row = ancestors.shape[0]
    a_col = ancestors.shape[1]
    block_size = ancestors.shape[2]
    count_s = panel_part.shape[0]
    row_at = lax.axis_index("row")
    col_at = lax.axis_index("col")
    root_count = a_col // a_row
    pieces = []
    for offset in range(root_count):
        pieces.append(spread(panel_part, "row", col_at * root_count + offset))
    column_panel = jnp.concatenate(pieces, axis=1)
    col_mask = lax.dynamic_slice_in_dim(present, col_at * a_col, a_col, 1)
    row_mask = lax.dynamic_slice_in_dim(present, row_at * a_row, a_row, 1)
    masked = column_panel * col_mask[:, :, None, None].astype(jnp.bfloat16)
    partial_sums = jnp.einsum(
        "ijab,kjbc->ikac", ancestors, masked, preferred_element_type=jnp.float32
    )
    term_blocks = -partial_sums * jnp.transpose(row_mask).astype(jnp.float32)[:, :, None, None]
    flat_terms = term_blocks.reshape(a_row * count_s, block_size, block_size)
    owned_blocks = lax.psum_scatter(flat_terms, "col", scatter_dimension=0, tiled=True)
    panel_flat = jnp.transpose(panel_part, (1, 0, 2, 3)).reshape(
        a_row * count_s, block_size, block_size
    )
    owned_count = owned_blocks.shape[0]
    first_row = col_at * owned_count
    panel_own = lax.dynamic_slice_in_dim(panel_flat, first_row, owned_count, 0)
    products = jnp.einsum(
        "nba,nbc->nac", panel_own.astype(jnp.float32), owned_blocks, precision=lax.Precision.HIGHEST
    )
    sup_index = (first_row + jnp.arange(owned_count, dtype=jnp.int32)) % count_s
    one_hot_rows = (sup_index[:, None] == jnp.arange(count_s, dtype=jnp.int32)[None, :]).astype(
        jnp.float32
    )
    diag_terms = jnp.einsum("nk,nac->kac", one_hot_rows, products, precision=lax.Precision.HIGHEST)
    diag_total = lax.psum(diag_terms, ("row", "col"))
    return (owned_blocks, inv_diag.astype(jnp.float32) - diag_total)


def body(ancestors, panel_one, present_one, dinv_one, panel_two, present_two, dinv_two):
    update_one, diag_one = one_level(ancestors, panel_one, present_one, dinv_one)
    update_two, diag_two = one_level(ancestors, panel_two, present_two, dinv_two)
    return (update_one, diag_one, update_two, diag_two)


def solution(mesh):
    in_specs = (
        P("row", "col", None, None),
        P(None, "row", None, None),
        P(),
        P(),
        P(None, "row", None, None),
        P(),
        P(),
    )
    out_specs = (P(("row", "col"), None, None), P(), P(("row", "col"), None, None), P())
    return jax.shard_map(body, mesh=mesh, in_specs=in_specs, out_specs=out_specs, check_vma=False)
```

profile of v0, /device:TPU:2, one launch (start us, length us, event | category | flops | bytes accessed | tf_op | source)
XLA Modules:
  0.0 787.7 jit_solution(2082607152326001342)
XLA Ops:
  7.2 0.0 all-reduce.7.cloned.1.call-start
  7.2 4.8 broadcast_select_fusion.6
  12.1 0.0 all-reduce.7.cloned.1.call-update
  12.1 0.0 reduce-scatter.5.cloned.1.call-start
  12.1 0.6 copy-done.4
  12.7 0.1 fusion.40
  12.8 0.1 fusion.42
  12.9 299.0 %all-reduce.7.cloned.1.call-done = (bf16[2,4,256,256]{3,2,1,0:T(8,128)(2,1)}, bf16[2,4,256,256]{3,2,1,0:T(8,128)(2,1)}, bf16[2,4,256,256]{3,2,1,0:T(8,128)(2,1)}...) async-done(((bf16[2,4,256,256]{3,2,1,0:T(8,128)(2,1)}, ...) | async-done | bytes 8388624 | tf_op jit(solution)/shard_map/psum | solution.py:9
  311.9 10.0 %bitcast_multiply_fusion = f32[4,2,256,256]{2,3,0,1:T(8,128)S(1)} fusion(bf16[4,16,256,256]{3,2,1,0:T(8,128)(2,1)} %param.7, bf16[2,4,256,256]{3,2,1,0:T(8,128)(2,1)} %get-tuple-element.10, bf16[2,4,256,256]{3,2,1,0:T(8,128)(2,1)} %get-tuple-element.11, bf16[2,4,256,256]{3,2,1,0:T(8,128)(2,1)} %get-tuple-element.12, ...), kind=kOutput, calls=%fused_computation.20 | convolution fusion | flops 4316987392 | bytes 14680160 | tf_op jit(solution)/shard_map/ijab,kjbc->ikac/dot_general | solution.py:27
  321.9 1.8 copy.17
  323.8 0.0 reduce-scatter.3.cloned.1.call-start
  323.8 11.3 %bitcast_multiply_fusion.1 = f32[4,2,256,256]{2,3,0,1:T(8,128)} fusion(bf16[4,16,256,256]{3,2,1,0:T(8,128)(2,1)} %param.7, bf16[2,4,256,256]{3,2,1,0:T(8,128)(2,1)S(1)} %copy-done.6, bf16[2,4,256,256]{3,2,1,0:T(8,128)(2,1)} %get-tuple-element.7, bf16[2,4,256,256]{3,2,1,0:T(8,128)(2,1)} %get-tuple-element.8, bf16[2,4,256,256]{3,2,1,0:T(8,128)(2,1)} %get-tuple-element.9, ...), kind=kOutput, calls=%fused_computation.22 | convolution fusion | flops 4316987392 | bytes 14680160 | tf_op jit(solution)/shard_map/ijab,kjbc->ikac/dot_general | solution.py:27
  335.2 3.1 copy.14
  338.3 0.0 all-reduce.5.cloned.1.call-start
  338.3 0.1 copy.18
  338.4 0.1 copy.15
  338.5 84.9 %reduce-scatter.5.cloned.1.call-done = f32[1,256,256]{2,1,0:T(8,128)} async-done(((f32[8,256,256]{2,1,0:T(8,128)}), f32[1,256,256]{2,1,0:T(8,128)}) %reduce-scatter.5.cloned.1.call-update) | async-done | bytes 262160 | tf_op jit(solution)/shard_map/reduce_scatter | solution.py:32
  423.4 1.3 fusion.30
  424.7 94.8 %reduce-scatter.3.cloned.1.call-done = f32[1,256,256]{2,1,0:T(8,128)} async-done(((f32[8,256,256]{2,1,0:T(8,128)}), f32[1,256,256]{2,1,0:T(8,128)}) %reduce-scatter.3.cloned.1.call-update) | async-done | bytes 262160 | tf_op jit(solution)/shard_map/reduce_scatter | solution.py:32
  519.5 1.3 fusion.32
  520.7 1.1 broadcast_multiply_fusion
  521.9 255.5 %all-reduce.5.cloned.1.call-done = (f32[2,256,256]{2,1,0:T(8,128)}, f32[2,256,256]{2,1,0:T(8,128)}) async-done(((f32[2,256,256]{2,1,0:T(8,128)}, f32[2,256,256]{2,1,0:T(8,128)}), (f32[2,256,256]{2,1,0:T(8,128)}, f32[2,256,256]{2,1,0:T(8,128)})) %all-reduce.5.cloned.1.call-update) | async-done | bytes 1048592 | tf_op jit(solution)/shard_map/psum | solution.py:47
  777.4 1.9 convert_subtract_fusion
  779.3 1.9 convert_subtract_fusion.1
  (17 shorter events, 0.1 us)
Async XLA Ops:
  7.2 304.7 %all-reduce.7.cloned.1.call-start = ((), (), s32[]{:S(2)}) async-start(), calls=%async_computation.5 | async-start | bytes 16777216 | tf_op jit(solution)/shard_map/psum | solution.py:9
  12.0 0.7 copy-start.4
  12.0 0.7 copy-start.5
  12.1 411.3 %reduce-scatter.5.cloned.1.call-start = ((), (), s32[]{:S(2)}) async-start(), calls=%async_computation.3 | async-start | bytes 2359296 | tf_op jit(solution)/shard_map/reduce_scatter | solution.py:32
  321.9 1.9 copy-start.6
  323.8 195.7 %reduce-scatter.3.cloned.1.call-start = ((), (), s32[]{:S(2)}) async-start(), calls=%async_computation.2 | async-start | bytes 2359296 | tf_op jit(solution)/shard_map/reduce_scatter | solution.py:32
  335.2 3.2 copy-start
  335.2 3.2 copy-start.1
  338.3 439.1 %copy-start.2 = (bf16[2,256,256]{2,1,0:T(8,128)(2,1)S(1)}, bf16[2,256,256]{2,1,0:T(8,128)(2,1)}, u32[]{:S(2)}) copy-start(bf16[2,256,256]{2,1,0:T(8,128)(2,1)} %param.13) | copy-start | bytes 786436
  338.3 439.1 %all-reduce.5.cloned.1.call-start = ((), (), s32[]{:S(2)}) async-start(), calls=%async_computation.4 | async-start | bytes 2097152 | tf_op jit(solution)/shard_map/psum | solution.py:47
  338.5 440.8 %copy-start.3 = (bf16[2,256,256]{2,1,0:T(8,128)(2,1)S(1)}, bf16[2,256,256]{2,1,0:T(8,128)(2,1)}, u32[]{:S(2)}) copy-start(bf16[2,256,256]{2,1,0:T(8,128)(2,1)} %param.10) | copy-start | bytes 786436
Sparse Core Ops, SparseCore 0:
  12.2 299.6 all-reduce.6
  323.9 99.4 reduce-scatter.4
  428.6 90.8 reduce-scatter.2
  525.5 251.8 all-reduce.4
where the time goes:
time: 788 us
  waiting for transfers between devices  734 us (93%)
  matrix products  23.8 us (3%)
  between operations  13.9 us (2%)
  other arithmetic  9.86 us (1%)
    psum x1, waiting for transfers between devices, spread(): return lax.psum(block, axis)  299 us
    psum x1, waiting for transfers between devices, one_level(): diag_total = lax.psum(diag_terms, ('row', 'col'))  256 us
    reduce_scatter x2, waiting for transfers between devices, one_level(): lax.psum_scatter(flat_terms, 'col', scatter_dimension=0, tiled=True)  180 us
    dot_general x2, matrix products, one_level(): jnp.einsum('ijab,kjbc->ikac', ancestors, masked, preferred_element_type=j...  21.3 us
  transfers between devices with their start and end apart: 4, of which 4 were waited for; matrix products, arithmetic and copies ran while one was open for 2% of the time, Pallas kernels for 0%

commit v1 on v0

--- a/solution.py
+++ b/solution.py
@@ -44,7 +44,8 @@
         jnp.float32
     )
     diag_terms = jnp.einsum("nk,nac->kac", one_hot_rows, products, precision=lax.Precision.HIGHEST)
-    diag_total = lax.psum(diag_terms, ("row", "col"))
+    set_task_here = lambda page: lax.psum(lax.psum(page, axis_name="row"), axis_name="col")
+    diag_total = set_task_here(diag_terms)
     return (owned_blocks, inv_diag.astype(jnp.float32) - diag_total)
 
 

time: 788 us -> 922 us (1.17)
  waiting for transfers between devices: 734 us -> 868 us
    psum x1 -> x2, waiting for transfers between devices: 256 us -> 389 us  [the longest x1 269 us: one_level(): lax.psum(page, axis_name='row')]
  transfers between devices with their start and end apart: 4 -> 5, of which waited for: 4 -> 5; matrix products, arithmetic and copies ran while one was open for 2% -> 2% of each run, Pallas kernels for 0% -> 0%
where the time goes in v1:
time: 922 us; the launch traced here: 921 us
  waiting for transfers between devices  868 us (94%)
  matrix products  23.8 us (3%)
  between operations  13.9 us (2%)
  other arithmetic  9.85 us (1%)
    psum x1, waiting for transfers between devices, spread(): return lax.psum(block, axis)  299 us
    psum x1, waiting for transfers between devices, one_level(): lax.psum(page, axis_name='row')  269 us
    reduce_scatter x2, waiting for transfers between devices, one_level(): lax.psum_scatter(flat_terms, 'col', scatter_dimension=0, tiled=True)  180 us
    psum x1, waiting for transfers between devices, one_level(): lax.psum(lax.psum(page, axis_name='row'), axis_name='col')  120 us
    dot_general x2, matrix products, one_level(): jnp.einsum('ijab,kjbc->ikac', ancestors, masked, preferred_element_type=j...  21.3 us
  transfers between devices with their start and end apart: 5, of which 5 were waited for; matrix products, arithmetic and copies ran while one was open for 2% of the time, Pallas kernels for 0%

profile of v1, /device:TPU:2, one launch (start us, length us, event | category | flops | bytes accessed | tf_op | source)
XLA Modules:
  0.0 921.4 jit_solution(11884126976590032399)
XLA Ops:
  7.2 4.8 broadcast_select_fusion.6
  12.1 0.0 reduce-scatter.5.cloned.1.call-start
  12.1 0.6 copy-done.4
  12.7 0.1 fusion.40
  12.8 0.1 fusion.42
  12.9 299.0 %all-reduce.11.cloned.1.call-done = (bf16[2,4,256,256]{3,2,1,0:T(8,128)(2,1)}, bf16[2,4,256,256]{3,2,1,0:T(8,128)(2,1)}, bf16[2,4,256,256]{3,2,1,0:T(8,128)(2,1)...) async-done(((bf16[2,4,256,256]{3,2,1,0:T(8,128)(2,1)}, ...) | async-done | bytes 8388624 | tf_op jit(solution)/shard_map/psum | solution.py:9
  311.9 10.0 %bitcast_multiply_fusion = f32[4,2,256,256]{2,3,0,1:T(8,128)S(1)} fusion(bf16[4,16,256,256]{3,2,1,0:T(8,128)(2,1)} %param.7, bf16[2,4,256,256]{3,2,1,0:T(8,128)(2,1)} %get-tuple-element.12, bf16[2,4,256,256]{3,2,1,0:T(8,128)(2,1)} %get-tuple-element.13, bf16[2,4,256,256]{3,2,1,0:T(8,128)(2,1)} %get-tuple-element.14, ...), kind=kOutput, calls=%fused_computation.20 | convolution fusion | flops 4316987392 | bytes 14680160 | tf_op jit(solution)/shard_map/ijab,kjbc->ikac/dot_general | solution.py:27
  321.9 1.8 copy.17
  323.8 0.0 reduce-scatter.3.cloned.1.call-start
  323.8 11.4 %bitcast_multiply_fusion.1 = f32[4,2,256,256]{2,3,0,1:T(8,128)} fusion(bf16[4,16,256,256]{3,2,1,0:T(8,128)(2,1)} %param.7, bf16[2,4,256,256]{3,2,1,0:T(8,128)(2,1)S(1)} %copy-done.6, bf16[2,4,256,256]{3,2,1,0:T(8,128)(2,1)} %get-tuple-element.9, bf16[2,4,256,256]{3,2,1,0:T(8,128)(2,1)} %get-tuple-element.10, ...), kind=kOutput, calls=%fused_computation.22 | convolution fusion | flops 4316987392 | bytes 14680160 | tf_op jit(solution)/shard_map/ijab,kjbc->ikac/dot_general | solution.py:27
  335.2 3.1 copy.14
  338.3 0.0 all-reduce.7.cloned.1.call-start
  338.3 0.1 copy.18
  338.4 0.1 copy.15
  338.5 84.9 %reduce-scatter.5.cloned.1.call-done = f32[1,256,256]{2,1,0:T(8,128)} async-done(((f32[8,256,256]{2,1,0:T(8,128)}), f32[1,256,256]{2,1,0:T(8,128)}) %reduce-scatter.5.cloned.1.call-update) | async-done | bytes 262160 | tf_op jit(solution)/shard_map/reduce_scatter | solution.py:32
  423.5 1.3 fusion.30
  424.7 94.8 %reduce-scatter.3.cloned.1.call-done = f32[1,256,256]{2,1,0:T(8,128)} async-done(((f32[8,256,256]{2,1,0:T(8,128)}), f32[1,256,256]{2,1,0:T(8,128)}) %reduce-scatter.3.cloned.1.call-update) | async-done | bytes 262160 | tf_op jit(solution)/shard_map/reduce_scatter | solution.py:32
  519.6 1.3 fusion.32
  520.8 1.1 broadcast_multiply_fusion
  522.0 0.0 all-reduce.9.cloned.1.call-start
  522.0 269.4 %all-reduce.7.cloned.1.call-done = (f32[2,256,256]{2,1,0:T(8,128)}, f32[2,256,256]{2,1,0:T(8,128)}) async-done(((f32[2,256,256]{2,1,0:T(8,128)}, f32[2,256,256]{2,1,0:T(8,128)}), (f32[2,256,256]{2,1,0:T(8,128)}, f32[2,256,256]{2,1,0:T(8,128)})) %all-reduce.7.cloned.1.call-update) | async-done | bytes 1048592 | tf_op jit(solution)/shard_map/psum | solution.py:47
  791.5 119.6 %all-reduce.9.cloned.1.call-done = (f32[2,256,256]{2,1,0:T(8,128)}, f32[2,256,256]{2,1,0:T(8,128)}) async-done(((f32[2,256,256]{2,1,0:T(8,128)}, f32[2,256,256]{2,1,0:T(8,128)}), (f32[2,256,256]{2,1,0:T(8,128)}, f32[2,256,256]{2,1,0:T(8,128)})) %all-reduce.9.cloned.1.call-update) | async-done | bytes 1048592 | tf_op jit(solution)/shard_map/psum | solution.py:47
  911.1 1.9 convert_subtract_fusion
  913.0 1.9 convert_subtract_fusion.1
  (20 shorter events, 0.2 us)
Async XLA Ops:
  7.2 304.7 %all-reduce.11.cloned.1.call-start = ((), (), s32[]{:S(2)}) async-start(), calls=%async_computation.6 | async-start | bytes 16777216 | tf_op jit(solution)/shard_map/psum | solution.py:9
  12.0 0.7 copy-start.4
  12.0 0.7 copy-start.5
  12.1 411.4 %reduce-scatter.5.cloned.1.call-start = ((), (), s32[]{:S(2)}) async-start(), calls=%async_computation.3 | async-start | bytes 2359296 | tf_op jit(solution)/shard_map/reduce_scatter | solution.py:32
  321.9 1.9 copy-start.6
  323.8 195.8 %reduce-scatter.3.cloned.1.call-start = ((), (), s32[]{:S(2)}) async-start(), calls=%async_computation.2 | async-start | bytes 2359296 | tf_op jit(solution)/shard_map/reduce_scatter | solution.py:32
  335.2 3.2 copy-start
  335.2 3.3 copy-start.1
  338.3 453.2 %all-reduce.7.cloned.1.call-start = ((), (), s32[]{:S(2)}) async-start(), calls=%async_computation.4 | async-start | bytes 2097152 | tf_op jit(solution)/shard_map/psum | solution.py:47
  338.3 572.8 %copy-start.2 = (bf16[2,256,256]{2,1,0:T(8,128)(2,1)S(1)}, bf16[2,256,256]{2,1,0:T(8,128)(2,1)}, u32[]{:S(2)}) copy-start(bf16[2,256,256]{2,1,0:T(8,128)(2,1)} %param.13) | copy-start | bytes 786436
  338.5 574.5 %copy-start.3 = (bf16[2,256,256]{2,1,0:T(8,128)(2,1)S(1)}, bf16[2,256,256]{2,1,0:T(8,128)(2,1)}, u32[]{:S(2)}) copy-start(bf16[2,256,256]{2,1,0:T(8,128)(2,1)} %param.10) | copy-start | bytes 786436
  522.0 389.2 %all-reduce.9.cloned.1.call-start = ((), (), s32[]{:S(2)}) async-start(), calls=%async_computation.5 | async-start | bytes 2097152 | tf_op jit(solution)/shard_map/psum | solution.py:47
Sparse Core Ops, SparseCore 0:
  12.2 299.6 all-reduce.10
  323.9 99.5 reduce-scatter.4
  428.7 90.8 reduce-scatter.2
  522.6 268.7 all-reduce.6
  794.2 116.8 all-reduce.8
